TPU v7x, 128 devices: a whole 4x4x4 slice. The times are simulated.
128 devices in a mesh: req: 32 (over x, z, core), mlp: 4 (over y).
Axes of the slice: x: 4, y: 4, z: 4, core: 2. Of those that a mesh axis runs over, the one named last changes fastest.
Arguments:
- tokens: bfloat16 [4096, 3584], P('req'), may hold values from -40 to 40
- segment_ids: int32 [32, 128], P('req'), may hold values from 0 to 3, never falling along the last dimension, each value on 1 to 64 neighbouring positions
- past_len: int32 [32, 4], P('req'), may hold values from 0 to 2047
- page_table: int32 [32, 64], P('req'), may hold values from 0 to 63, each once within a row
- migrate_pages: int32 [32, 32, 1], P('req'), may hold values from 0 to 31
- pooled_key_cache: bfloat16 [1024, 64, 1024], P('req', None, 'mlp'), may hold values from -6 to 6
- pooled_value_cache: bfloat16 [1024, 64, 1024], P('req', None, 'mlp'), may hold values from -6 to 6
- attn_gain: float32 [3584], replicated, may hold values from 0.25 to 1.75
- w_query: bfloat16 [3584, 2048], P(None, 'mlp'), may hold values from -0.09375 to 0.09375
- key_matrix: bfloat16 [3584, 1024], P(None, 'mlp'), may hold values from -0.09375 to 0.09375
- value_matrix: bfloat16 [3584, 1024], P(None, 'mlp'), may hold values from -0.09375 to 0.09375
- w_out: bfloat16 [2048, 3584], P('mlp'), may hold values from -1 to 1
- post_attn_gain: float32 [3584], replicated, may hold values from 0.25 to 1.75
- ffw_gain: float32 [3584], replicated, may hold values from 0.25 to 1.75
- w_gate: bfloat16 [3584, 14336], P(None, 'req'), may hold values from -0.09375 to 0.09375
- w_up: bfloat16 [3584, 14336], P(None, 'req'), may hold values from -0.09375 to 0.09375
- w_down: bfloat16 [14336, 3584], P('req'), may hold values from -1 to 1
- post_ffw_gain: float32 [3584], replicated, may hold values from 0.25 to 1.75
Outputs:
- mixed: bfloat16 [4096, 3584], P(('req', 'mlp'))
- written_key_rows: bfloat16 [4096, 1024], P('req', 'mlp')
- written_value_rows: bfloat16 [4096, 1024], P('req', 'mlp')
Inputs may be any that keep to these rules, and one draw needn't show every extreme that they name: `segment_ids`: in each row the requests 0 to 3 appear in order; each request has 1 to 64 new tokens, and some request exactly 64. `page_table`: each row is a permutation; every page of the owner's list (own pool and received pages) lies in exactly one request's window. `migrate_pages`: entry [s, d, m] names a page of owner s's pool.
All inputs are finite; a program needn't handle non-finite values.
Results may differ from a plain program's by a relative error of at most 0.015.
Values may be sent and summed in bfloat16 or wider, within the bound.
No kernel may reach another device: no remote copies, remote signals or barrier semaphores. Data moves between devices by JAX's collectives and lax.ppermute only.
A program may use at most 128 MiB of HBM per device.

v0:
```python
import jax
import jax.numpy as jnp
from jax import lax
from jax.sharding import PartitionSpec as P

HEAD_SIZE = 256
WINDOW_LENGTH = 1024
SOFT_CAP = 50.0
NORM_EPS = 1e-06
ROPE_BASE = 10000.0


def rms_scale(values, gain):
    return values * lax.rsqrt(jnp.mean(values * values, axis=-1, keepdims=True) + NORM_EPS) * gain


def apply_rotary(vectors, token_positions):
    width = vectors.shape[-1]
    half = width // 2
    frequency = ROPE_BASE ** (-jnp.arange(half, dtype=jnp.float32) * (2.0 / width))
    angles = token_positions.astype(jnp.float32)[:, None] * frequency[None, :]
    cosine = jnp.cos(angles)[:, None, :]
    sine = jnp.sin(angles)[:, None, :]
    first = vectors[..., :half]
    second = vectors[..., half:]
    return jnp.concatenate(
        [first * cosine - second * sine, second * cosine + first * sine], axis=-1
    )


def token_layout(segment, past):
    requests = jnp.arange(past.shape[0], dtype=jnp.int32)
    member = segment[:, None] == requests[None, :]
    firsts = jnp.sum((segment[:, None] < requests[None, :]).astype(jnp.int32), axis=0)
    offsets = jnp.arange(segment.shape[0], dtype=jnp.int32) - jnp.sum(
        jnp.where(member, firsts[None, :], 0), axis=1
    )
    token_positions = jnp.sum(jnp.where(member, past[None, :], 0), axis=1) + offsets
    return (offsets, token_positions)


def visibility(segment, offsets, past, window):
    count_req = past.shape[0]
    requests = jnp.arange(count_req, dtype=jnp.int32)
    slots = jnp.arange(count_req * window, dtype=jnp.int32)
    slot_req = slots // window
    slot_pos = slots % window
    slot_past = jnp.sum(jnp.where(slot_req[:, None] == requests[None, :], past[None, :], 0), axis=1)
    cached = (
        (segment[:, None] == slot_req[None, :])
        & (slot_pos[None, :] > offsets[:, None])
        & (slot_pos[None, :] >= window - slot_past[None, :])
    )
    order = jnp.arange(segment.shape[0], dtype=jnp.int32)
    fresh = (segment[:, None] == segment[None, :]) & (order[None, :] <= order[:, None])
    return (cached, fresh)


def local(
    tokens,
    segment_ids,
    past_len,
    page_table,
    migrate_pages,
    pooled_key_cache,
    pooled_value_cache,
    attn_gain,
    w_query,
    key_matrix,
    value_matrix,
    w_out,
    post_attn_gain,
    ffw_gain,
    w_gate,
    w_up,
    w_down,
    post_ffw_gain,
):
    tok_count = tokens.shape[0]
    key_heads = key_matrix.shape[1] // HEAD_SIZE
    query_heads = w_query.shape[1] // HEAD_SIZE
    query_group = query_heads // key_heads
    scale = float(HEAD_SIZE) ** (-0.5)
    page_len = pooled_key_cache.shape[1]
    columns = pooled_key_cache.shape[2]
    send_list = migrate_pages[0]
    owners = send_list.shape[0]
    flat_list = send_list.reshape(-1)
    send_keys = jnp.take(pooled_key_cache, flat_list, axis=0).reshape(
        owners, send_list.shape[1], page_len, columns
    )
    send_values = jnp.take(pooled_value_cache, flat_list, axis=0).reshape(
        owners, send_list.shape[1], page_len, columns
    )
    recv_keys, recv_values = (
        lax.all_to_all(send_keys, "req", split_axis=0, concat_axis=0, tiled=True),
        lax.all_to_all(send_values, "req", split_axis=0, concat_axis=0, tiled=True),
    )
    page_lookup = page_table[0]
    listed_keys = jnp.concatenate(
        [pooled_key_cache, recv_keys.reshape(-1, page_len, columns)], axis=0
    )
    listed_values = jnp.concatenate(
        [pooled_value_cache, recv_values.reshape(-1, page_len, columns)], axis=0
    )
    window_keys = jnp.take(listed_keys, page_lookup, axis=0).reshape(-1, key_heads, HEAD_SIZE)
    window_values = jnp.take(listed_values, page_lookup, axis=0).reshape(-1, key_heads, HEAD_SIZE)
    segment = segment_ids[0]
    past = past_len[0]
    offsets, token_positions = token_layout(segment, past)
    normalized_input = rms_scale(tokens.astype(jnp.float32), attn_gain).astype(jnp.bfloat16)
    query_rows = apply_rotary(
        jnp.dot(normalized_input, w_query, preferred_element_type=jnp.float32).reshape(
            tok_count, query_heads, HEAD_SIZE
        ),
        token_positions,
    ).astype(jnp.bfloat16)
    incoming_keys = apply_rotary(
        jnp.dot(normalized_input, key_matrix, preferred_element_type=jnp.float32).reshape(
            tok_count, key_heads, HEAD_SIZE
        ),
        token_positions,
    ).astype(jnp.bfloat16)
    incoming_values = jnp.dot(
        normalized_input, value_matrix, preferred_element_type=jnp.float32
    ).astype(jnp.bfloat16)
    grouped_queries = query_rows.reshape(tok_count, key_heads, query_group, HEAD_SIZE)
    value_heads = incoming_values.reshape(tok_count, key_heads, HEAD_SIZE)
    score_cached = jnp.einsum(
        "tkgd,skd->tkgs", grouped_queries, window_keys, preferred_element_type=jnp.float32
    )
    score_fresh = jnp.einsum(
        "tkgd,skd->tkgs", grouped_queries, incoming_keys, preferred_element_type=jnp.float32
    )
    cached, fresh = visibility(segment, offsets, past, WINDOW_LENGTH)
    weight_cached = jnp.where(
        cached[:, None, None, :],
        jnp.exp(SOFT_CAP * jnp.tanh(score_cached * (scale / SOFT_CAP))),
        0.0,
    )
    weight_fresh = jnp.where(
        fresh[:, None, None, :], jnp.exp(SOFT_CAP * jnp.tanh(score_fresh * (scale / SOFT_CAP))), 0.0
    )
    totals = jnp.sum(weight_cached, axis=-1, keepdims=True) + jnp.sum(
        weight_fresh, axis=-1, keepdims=True
    )
    prob_cached = (weight_cached / totals).astype(jnp.bfloat16)
    prob_fresh = (weight_fresh / totals).astype(jnp.bfloat16)
    attended = jnp.einsum(
        "tkgs,skd->tkgd", prob_cached, window_values, preferred_element_type=jnp.float32
    )
    attended = attended + jnp.einsum(
        "tkgs,skd->tkgd", prob_fresh, value_heads, preferred_element_type=jnp.float32
    )
    attention = attended.astype(jnp.bfloat16).reshape(tok_count, query_heads * HEAD_SIZE)
    rows_mine = tok_count // lax.axis_size("mlp")
    attn_out = lax.psum_scatter(
        jnp.dot(attention, w_out, preferred_element_type=jnp.float32).astype(jnp.bfloat16),
        "mlp",
        scatter_dimension=0,
        tiled=True,
    ).astype(jnp.float32)
    own_rows = lax.dynamic_slice_in_dim(
        tokens, lax.axis_index("mlp") * rows_mine, rows_mine, 0
    ).astype(jnp.float32)
    residual_stream = own_rows + rms_scale(attn_out, post_attn_gain)
    feedforward_input = rms_scale(residual_stream, ffw_gain).astype(jnp.bfloat16)
    piece = lax.all_gather(feedforward_input, "req", axis=0, tiled=True)
    gate_part = jnp.dot(piece, w_gate, preferred_element_type=jnp.float32)
    up_part = jnp.dot(piece, w_up, preferred_element_type=jnp.float32)
    hidden = (jax.nn.gelu(gate_part, approximate=True) * up_part).astype(jnp.bfloat16)
    ffw_out = lax.psum_scatter(
        jnp.dot(hidden, w_down, preferred_element_type=jnp.float32).astype(jnp.bfloat16),
        "req",
        scatter_dimension=0,
        tiled=True,
    ).astype(jnp.float32)
    mixed = (residual_stream + rms_scale(ffw_out, post_ffw_gain)).astype(jnp.bfloat16)
    return (mixed, incoming_keys.reshape(tok_count, key_heads * HEAD_SIZE), incoming_values)


def solution(mesh):
    return jax.shard_map(
        local,
        mesh=mesh,
        in_specs=(
            P("req", None),
            P("req", None),
            P("req", None),
            P("req", None),
            P("req", None, None),
            P("req", None, "mlp"),
            P("req", None, "mlp"),
            P(),
            P(None, "mlp"),
            P(None, "mlp"),
            P(None, "mlp"),
            P("mlp", None),
            P(),
            P(),
            P(None, "req"),
            P(None, "req"),
            P("req", None),
            P(),
        ),
        out_specs=(P(("req", "mlp"), None), P("req", "mlp"), P("req", "mlp")),
        check_vma=False,
    )
```

profile of v0, /device:TPU:0, one launch (start us, length us, event | category | flops | bytes accessed | tf_op | source)
XLA Modules:
  0.0 282.2 jit_solution(7771821692837029242)
XLA Ops:
  8.8 2.8 gather_fusion.2
  11.6 2.9 %gather_fusion = bf16[32,64,256]{2,1,0:T(8,128)(2,1)} fusion(bf16[32,64,256]{2,1,0:T(8,128)(2,1)} %param.28, s32[1024]{0:T(1024)S(1)} %pad_clamp_fusion.1), kind=kCustom, calls=%fused_computation.clone | custom fusion | bytes 2097280 | tf_op jit(solution)/shard_map/jit(_take)/gather | solution.py:92
  14.5 3.1 %select_bitcast_fusion = (bf16[32,1,64,256]{3,2,1,0:T(8,128)(2,1)}, bf16[32,1,64,256]{3,2,1,0:T(8,128)(2,1)}) fusion(bf16[32,64,256]{2,1,0:T(8,128)(2,1)} %gather_fusion.2, pred[32]{0:T(512)(128)(4,1)S(1)} %compare_and_fusion.1, bf16[32,64,256]{2,1,0:T(8,128)(2,1)} %gather_fusion), kind=kLoop, calls=%fused_computation.45 | loop fusion | flops 1048576 | bytes 4194336 | tf_op jit(solution)/shard_map/reshape | solution.py:89
  17.6 8.5 %all-to-all-start = ((bf16[32,1,64,256]{3,2,1,0:T(8,128)(2,1)}), bf16[32,1,64,256]{3,2,1,0:T(8,128)(2,1)}, u32[]{:S(2)}, u32[]{:S(2)}) async-start(bf16[32,1,64,256]{3,2,1,0:T(8,128)(2,1)} %get-tuple-element.20), calls=%async_computation | async-start | bytes 2097152 | tf_op jit(solution)/shard_map/all_to_all | solution.py:97
  27.4 1.7 fusion.7
  32.3 2.2 convolution_bitcast_fusion
  39.6 1.7 fusion.61
  41.4 2.3 convolution_convert_fusion.2
  43.7 7.4 %all-to-all-start.1 = ((bf16[32,1,64,256]{3,2,1,0:T(8,128)(2,1)}), bf16[32,1,64,256]{3,2,1,0:T(8,128)(2,1)}, u32[]{:S(2)}, u32[]{:S(2)}) async-start(bf16[32,1,64,256]{3,2,1,0:T(8,128)(2,1)} %get-tuple-element.19), calls=%async_computation.1 | async-start | bytes 2097152 | tf_op jit(solution)/shard_map/all_to_all | solution.py:96
  51.2 4.6 %and_and_fusion = pred[128,4096]{0,1:T(8,128)(4,1)} fusion(s32[128]{0:T(128)S(1)} %copy-done.13, s32[128]{0:T(128)S(1)} %bitcast.86, s32[4096]{0:T(1024)S(1)} %copy-done.6, s32[4096]{0:T(1024)S(1)} %get-tuple-element.26, pred[4096]{0:T(1024)(128)(4,1)S(1)} %copy-done.8), kind=kLoop, calls=%fused_computation.22 | loop fusion | flops 2097152 | bytes 562176 | tf_op jit(solution)/shard_map/and | solution.py:50
  55.8 3.0 %pad_maximum_fusion = bf16[64,64,256]{2,1,0:T(8,128)(2,1)} fusion(bf16[32,64,256]{2,1,0:T(8,128)(2,1)} %bitcast.3, bf16[32,64,256]{2,1,0:T(8,128)(2,1)} %param.28), kind=kLoop, calls=%fused_computation.16 | loop fusion | flops 1048576 | bytes 4194304 | tf_op jit(solution)/shard_map/concatenate | solution.py:103
  58.9 9.0 %all-to-all-done.1 = bf16[32,1,64,256]{3,2,1,0:T(8,128)(2,1)} async-done(((bf16[32,1,64,256]{3,2,1,0:T(8,128)(2,1)}), bf16[32,1,64,256]{3,2,1,0:T(8,128)(2,1)}, u32[]{:S(2)}, u32[]{:S(2)}) %all-to-all-start.1) | async-done | bytes 1048608 | tf_op jit(solution)/shard_map/all_to_all | solution.py:96
  67.9 3.1 %pad_maximum_fusion.1 = bf16[64,64,256]{2,1,0:T(8,128)(2,1)} fusion(bf16[32,64,256]{2,1,0:T(8,128)(2,1)} %bitcast.9, bf16[32,64,256]{2,1,0:T(8,128)(2,1)} %param.27), kind=kLoop, calls=%fused_computation.17 | loop fusion | flops 1048576 | bytes 4194304 | tf_op jit(solution)/shard_map/concatenate | solution.py:100
  71.0 3.7 %gather_fusion.1 = bf16[64,64,256]{2,1,0:T(8,128)(2,1)} fusion(bf16[64,64,256]{2,1,0:T(8,128)(2,1)} %pad_maximum_fusion, s32[1024]{0:T(1024)} %pad_clamp_fusion), kind=kCustom, calls=%fused_computation.1.clone | custom fusion | bytes 4194560 | tf_op jit(solution)/shard_map/jit(_take)/gather | solution.py:107
  74.7 3.7 %gather_fusion.3 = bf16[64,64,256]{2,1,0:T(8,128)(2,1)} fusion(bf16[64,64,256]{2,1,0:T(8,128)(2,1)} %pad_maximum_fusion.1, s32[1024]{0:T(1024)} %pad_clamp_fusion), kind=kCustom, calls=%fused_computation.3.clone | custom fusion | bytes 4194560 | tf_op jit(solution)/shard_map/jit(_take)/gather | solution.py:106
  78.4 2.7 broadcast_select_fusion
  84.6 1.6 convolution_convert_fusion.1
  86.3 21.4 %reduce-scatter.3.cloned.1.call-done = bf16[32,3584]{1,0:T(8,128)(2,1)} async-done(((bf16[128,3584]{1,0:T(8,128)(2,1)}), bf16[32,3584]{1,0:T(8,128)(2,1)}) %reduce-scatter.3.cloned.1.call-update) | async-done | bytes 229392 | tf_op jit(solution)/shard_map/reduce_scatter | solution.py:157
  110.2 1.9 multiply_convert_fusion
  112.4 50.6 %all-gather.2.cloned.1.call-done = bf16[1024,3584]{1,0:T(8,128)(2,1)} async-done(((bf16[32,3584]{1,0:T(8,128)(2,1)}), bf16[1024,3584]{1,0:T(8,128)(2,1)}) %all-gather.2.cloned.1.call-update) | async-done | bytes 7340048 | tf_op jit(solution)/shard_map/all_gather | solution.py:168
  162.9 8.7 %fusion.62 = f32[1024,448]{0,1:T(8,128)} fusion(bf16[1024,3584]{1,0:T(8,128)(2,1)} %all-gather.2.cloned.1.call-done, bf16[3584,448]{0,1:T(8,128)(2,1)} %param.36), kind=kOutput, calls=%fused_computation.122 | convolution fusion | flops 3288334336 | bytes 12386304 | tf_op jit(solution)/shard_map/dot_general | solution.py:169
  171.7 13.0 %convolution_convert_fusion = bf16[1024,3584]{1,0:T(8,128)(2,1)} fusion(bf16[448,3584]{1,0:T(8,128)(2,1)S(1)} %copy-done, f32[1024,448]{0,1:T(8,128)} %fusion.62, bf16[1024,3584]{1,0:T(8,128)(2,1)} %all-gather.2.cloned.1.call-done, bf16[3584,448]{0,1:T(8,128)(2,1)} %param.37), kind=kOutput, calls=%fused_computation.4 | convolution fusion | flops 6584926208 | bytes 22937600 | tf_op jit(solution)/shard_map/dot_general | solution.py:173
  184.8 87.8 %reduce-scatter.5.cloned.1.call-done = bf16[32,3584]{1,0:T(8,128)(2,1)} async-done(((bf16[1024,3584]{1,0:T(8,128)(2,1)}), bf16[32,3584]{1,0:T(8,128)(2,1)}) %reduce-scatter.5.cloned.1.call-update) | async-done | bytes 229392 | tf_op jit(solution)/shard_map/reduce_scatter | solution.py:172
  273.7 2.0 fusion.31
  (81 shorter events, 18.4 us)
Async XLA Ops:
  7.2 164.5 %copy-start = (bf16[448,3584]{1,0:T(8,128)(2,1)S(1)}, bf16[448,3584]{1,0:T(8,128)(2,1)}, u32[]{:S(2)}) copy-start(bf16[448,3584]{1,0:T(8,128)(2,1)} %param.38) | copy-start | bytes 9633796
  17.6 8.6 %copy-start.17 = (s32[1,64]{1,0:T(1,128)S(1)}, s32[1,64]{1,0:T(1,128)}, u32[]{:S(2)}) copy-start(s32[1,64]{1,0:T(1,128)} %param.25) | copy-start | bytes 772
  17.6 11.5 %copy-start.10 = (s32[1,128]{1,0:T(1,128)S(1)}, s32[1,128]{1,0:T(1,128)}, u32[]{:S(2)}) copy-start(s32[1,128]{1,0:T(1,128)} %param.23) | copy-start | bytes 1540
  17.6 12.2 %copy-start.12 = (s32[1,4]{1,0:T(1,128)S(1)}, s32[1,4]{1,0:T(1,128)}, u32[]{:S(2)}) copy-start(s32[1,4]{1,0:T(1,128)} %param.24) | copy-start | bytes 52
  17.6 14.7 %copy-start.16 = (f32[3584]{0:T(1024)S(1)}, f32[3584]{0:T(1024)}, u32[]{:S(2)}) copy-start(f32[3584]{0:T(1024)} %param.29) | copy-start | bytes 43012
  17.6 26.0 %all-to-all-start = ((bf16[32,1,64,256]{3,2,1,0:T(8,128)(2,1)}), bf16[32,1,64,256]{3,2,1,0:T(8,128)(2,1)}, u32[]{:S(2)}, u32[]{:S(2)}) async-start(bf16[32,1,64,256]{3,2,1,0:T(8,128)(2,1)} %get-tuple-element.20), calls=%async_computation | async-start | bytes 2097152 | tf_op jit(solution)/shard_map/all_to_all | solution.py:97
  26.8 8.1 %copy-start.15 = (bf16[3584,512]{1,0:T(8,128)(2,1)S(1)}, bf16[3584,512]{1,0:T(8,128)(2,1)}, u32[]{:S(2)}) copy-start(bf16[3584,512]{1,0:T(8,128)(2,1)} %param.30) | copy-start | bytes 11010052
  27.4 7.5 %copy-start.3 = (bf16[128,3584]{1,0:T(8,128)(2,1)S(1)}, bf16[128,3584]{1,0:T(8,128)(2,1)}, u32[]{:S(2)}) copy-start(bf16[128,3584]{1,0:T(8,128)(2,1)} %param.22) | copy-start | bytes 2752516
  29.1 7.1 %copy-start.20 = (f32[128]{0:T(128)}, f32[128]{0:T(128)S(1)}, u32[]{:S(2)}) copy-start(f32[128]{0:T(128)S(1)} %add_rsqrt_fusion.3) | copy-start | bytes 1540
  41.4 9.8 %copy-start.6 = (s32[4096]{0:T(1024)S(1)}, s32[4096]{0:T(1024)}, u32[]{:S(2)}) copy-start(s32[4096]{0:T(1024)} %get-tuple-element.25) | copy-start | bytes 49156
  41.4 9.8 %copy-start.8 = (pred[4096]{0:T(1024)(128)(4,1)S(1)}, pred[4096]{0:T(1024)(128)(4,1)}, u32[]{:S(2)}) copy-start(pred[4096]{0:T(1024)(128)(4,1)} %subtract_compare_fusion) | copy-start | bytes 12292
  41.4 9.8 %copy-start.11 = (s32[1,128]{1,0:T(1,128)S(1)}, s32[1,128]{1,0:T(1,128)}, u32[]{:S(2)}) copy-start(s32[1,128]{1,0:T(1,128)} %param.23) | copy-start | bytes 1540
  41.4 9.8 %copy-start.13 = (s32[128]{0:T(128)S(1)}, s32[128]{0:T(128)}, u32[]{:S(2)}) copy-start(s32[128]{0:T(128)} %get-tuple-element.16) | copy-start | bytes 1540
  43.6 39.7 %copy-start.18 = (bf16[128,256]{1,0:T(8,128)(2,1)}, bf16[128,256]{1,0:T(8,128)(2,1)S(1)}, u32[]{:S(2)}) copy-start(bf16[128,256]{1,0:T(8,128)(2,1)S(1)} %convolution_convert_fusion.2) | copy-start | bytes 196612
  43.7 24.2 %all-to-all-start.1 = ((bf16[32,1,64,256]{3,2,1,0:T(8,128)(2,1)}), bf16[32,1,64,256]{3,2,1,0:T(8,128)(2,1)}, u32[]{:S(2)}, u32[]{:S(2)}) async-start(bf16[32,1,64,256]{3,2,1,0:T(8,128)(2,1)} %get-tuple-element.19), calls=%async_computation.1 | async-start | bytes 2097152 | tf_op jit(solution)/shard_map/all_to_all | solution.py:96
  51.1 56.6 %reduce-scatter.3.cloned.1.call-start = ((), (), s32[]{:S(2)}) async-start(), calls=%async_computation.4 | async-start | bytes 1146880 | tf_op jit(solution)/shard_map/reduce_scatter | solution.py:157
  74.7 3.7 %copy-start.14 = (pred[64]{0:T(512)(128)(4,1)S(1)}, pred[64]{0:T(512)(128)(4,1)}, u32[]{:S(2)}) copy-start(pred[64]{0:T(512)(128)(4,1)} %compare_and_fusion) | copy-start | bytes 196
  78.4 2.7 copy-start.4
  84.6 24.2 %copy-start.5 = (f32[3584]{0:T(1024)S(1)}, f32[3584]{0:T(1024)}, u32[]{:S(2)}) copy-start(f32[3584]{0:T(1024)} %param.34) | copy-start | bytes 43012
  84.6 25.5 %copy-start.9 = (f32[3584]{0:T(1024)S(1)}, f32[3584]{0:T(1024)}, u32[]{:S(2)}) copy-start(f32[3584]{0:T(1024)} %param.35) | copy-start | bytes 43012
  86.3 76.7 %all-gather.2.cloned.1.call-start = ((), (), s32[]{:S(2)}) async-start(), calls=%async_computation.5 | async-start | bytes 7569408 | tf_op jit(solution)/shard_map/all_gather | solution.py:168
  112.1 160.4 %reduce-scatter.5.cloned.1.call-start = ((), (), s32[]{:S(2)}) async-start(), calls=%async_computation.6 | async-start | bytes 7569408 | tf_op jit(solution)/shard_map/reduce_scatter | solution.py:172
  184.7 89.0 %copy-start.2 = (bf16[32,3584]{1,0:T(8,128)(2,1)S(1)}, bf16[32,3584]{1,0:T(8,128)(2,1)}, u32[]{:S(2)}) copy-start(bf16[32,3584]{1,0:T(8,128)(2,1)} %reduce-scatter.3.cloned.1.call-done) | copy-start | bytes 688132
  184.7 89.0 %copy-start.7 = (f32[3584]{0:T(1024)S(1)}, f32[3584]{0:T(1024)}, u32[]{:S(2)}) copy-start(f32[3584]{0:T(1024)} %param.39) | copy-start | bytes 43012
  (2 other events, 3.0 us)
Sparse Core Ops, SparseCore 0:
  86.4 21.2 reduce-scatter.2
  112.2 50.6 all-gather.1
  184.9 87.6 reduce-scatter.4
where the time goes:
time: 283 us; the launch traced here: 282 us
  waiting for transfers between devices  169 us (60%)
  other arithmetic  34.1 us (12%)
  matrix products  33.4 us (12%)
  starting transfers between devices  16.3 us (6%)
  local copies, waits for them, and re-layouts  15.5 us (5%)
  between operations  14 us (5%)
    reduce_scatter x1, waiting for transfers between devices, local(): lax.psum_scatter(jnp.dot(hidden, w_down, preferred_element_type=jnp.float...  87.8 us
    all_gather x1, waiting for transfers between devices, local(): piece = lax.all_gather(feedforward_input, 'req', axis=0, tiled=True)  50.6 us
    reduce_scatter x1, waiting for transfers between devices, local(): lax.psum_scatter(jnp.dot(attention, w_out, preferred_element_type=jnp.flo...  21.4 us
    dot_general x1, matrix products, local(): jnp.dot(hidden, w_down, preferred_element_type=jnp.float32)  13 us
    all_to_all x1, waiting for transfers between devices, local(): lax.all_to_all(send_keys, 'req', split_axis=0, concat_axis=0, tiled=True)  9.04 us
    dot_general x1, matrix products, local(): gate_part = jnp.dot(piece, w_gate, preferred_element_type=jnp.float32)  8.75 us
    all_to_all x1, starting transfers between devices, local(): lax.all_to_all(send_values, 'req', split_axis=0, concat_axis=0, tiled=True)  8.52 us
    all_to_all x1, starting transfers between devices, local(): lax.all_to_all(send_keys, 'req', split_axis=0, concat_axis=0, tiled=True)  7.45 us
  transfers between devices with their start and end apart: 5, of which 4 were waited for; matrix products, arithmetic and copies ran while one was open for 9% of the time, Pallas kernels for 0%

commit v1 on v0

--- a/solution.py
+++ b/solution.py
@@ -8,6 +8,11 @@
 SOFT_CAP = 50.0
 NORM_EPS = 1e-06
 ROPE_BASE = 10000.0
+
+
+def exchange_gather(x, mesh_axis, dim):
+    repeated = jnp.stack([x] * lax.axis_size(mesh_axis))
+    return jnp.concatenate(lax.all_to_all(repeated, mesh_axis, 0, 0), axis=dim)
 
 
 def rms_scale(values, gain):
@@ -165,7 +170,7 @@
     ).astype(jnp.float32)
     residual_stream = own_rows + rms_scale(attn_out, post_attn_gain)
     feedforward_input = rms_scale(residual_stream, ffw_gain).astype(jnp.bfloat16)
-    piece = lax.all_gather(feedforward_input, "req", axis=0, tiled=True)
+    piece = exchange_gather(feedforward_input, "req", 0)
     gate_part = jnp.dot(piece, w_gate, preferred_element_type=jnp.float32)
     up_part = jnp.dot(piece, w_up, preferred_element_type=jnp.float32)
     hidden = (jax.nn.gelu(gate_part, approximate=True) * up_part).astype(jnp.bfloat16)

time: 283 us -> 321 us (1.13)
  blocking collectives: 0 us -> 91.5 us
  waiting for transfers between devices: 169 us -> 116 us
  matrix products: 33.4 us -> 29.4 us
  local copies, waits for them, and re-layouts: 15.5 us -> 19.3 us
    all_to_all x0 -> x1, blocking collectives: none -> 91.5 us  [exchange_gather(): return jnp.concatenate(lax.all_to_all(repeated, mesh_axis, 0, 0), axis=dim)]
    all_gather x1 -> x0, waiting for transfers between devices: 50.6 us -> none  [local(): piece = lax.all_gather(feedforward_input, 'req', axis=0, tiled=True)]
    dot_general x1, matrix products: 8.75 us -> 4.73 us  [local(): gate_part = jnp.dot(piece, w_gate, preferred_element_type=jnp.float32)]
  transfers between devices with their start and end apart: 5 -> 4, of which waited for: 4 -> 3; matrix products, arithmetic and copies ran while one was open for 9% -> 8% of each run, Pallas kernels for 0% -> 0%
where the time goes in v1:
time: 321 us; the launch traced here: 320 us
  waiting for transfers between devices  116 us (36%)
  blocking collectives  91.5 us (29%)
  other arithmetic  33.4 us (10%)
  matrix products  29.4 us (9%)
  local copies, waits for them, and re-layouts  19.3 us (6%)
  starting transfers between devices  16 us (5%)
  between operations  14.4 us (4%)
    all_to_all x1, blocking collectives, exchange_gather(): return jnp.concatenate(lax.all_to_all(repeated, mesh_axis, 0, 0), axis=dim)  91.5 us
    reduce_scatter x1, waiting for transfers between devices, local(): lax.psum_scatter(jnp.dot(hidden, w_down, preferred_element_type=jnp.float...  85.2 us
    reduce_scatter x1, waiting for transfers between devices, local(): lax.psum_scatter(jnp.dot(attention, w_out, preferred_element_type=jnp.flo...  21.4 us
    dot_general x1, matrix products, local(): jnp.dot(hidden, w_down, preferred_element_type=jnp.float32)  13 us
    all_to_all x1, waiting for transfers between devices, local(): lax.all_to_all(send_keys, 'req', split_axis=0, concat_axis=0, tiled=True)  9.02 us
    all_to_all x1, starting transfers between devices, local(): lax.all_to_all(send_values, 'req', split_axis=0, concat_axis=0, tiled=True)  8.52 us
    all_to_all x1, starting transfers between devices, local(): lax.all_to_all(send_keys, 'req', split_axis=0, concat_axis=0, tiled=True)  7.44 us
  transfers between devices with their start and end apart: 4, of which 3 were waited for; matrix products, arithmetic and copies ran while one was open for 8% of the time, Pallas kernels for 0%

profile of v1, /device:TPU:0, one launch (start us, length us, event | category | flops | bytes accessed | tf_op | source)
XLA Modules:
  0.0 319.7 jit_solution(863725572466236379)
XLA Ops:
  8.8 2.8 gather_fusion.2
  11.6 2.9 gather_fusion
  14.5 3.1 select_bitcast_fusion
  17.6 8.5 %all-to-all-start = ((bf16[32,1,64,256]{3,2,1,0:T(8,128)(2,1)}), bf16[32,1,64,256]{3,2,1,0:T(8,128)(2,1)}, u32[]{:S(2)}, u32[]{:S(2)}) async-start(bf16[32,1,64,256]{3,2,1,0:T(8,128)(2,1)} %get-tuple-element.20), calls=%async_computation | async-start | bytes 2097152 | tf_op jit(solution)/shard_map/all_to_all | solution.py:102
  27.3 1.7 fusion.7
  32.2 2.2 convolution_bitcast_fusion
  39.6 1.7 fusion.61
  41.3 2.3 convolution_convert_fusion.2
  43.6 7.4 %all-to-all-start.1 = ((bf16[32,1,64,256]{3,2,1,0:T(8,128)(2,1)}), bf16[32,1,64,256]{3,2,1,0:T(8,128)(2,1)}, u32[]{:S(2)}, u32[]{:S(2)}) async-start(bf16[32,1,64,256]{3,2,1,0:T(8,128)(2,1)} %get-tuple-element.19), calls=%async_computation.1 | async-start | bytes 2097152 | tf_op jit(solution)/shard_map/all_to_all | solution.py:101
  51.1 4.6 %and_and_fusion = pred[128,4096]{0,1:T(8,128)(4,1)} fusion(s32[128]{0:T(128)S(1)} %copy-done.14, s32[128]{0:T(128)S(1)} %bitcast.89, s32[4096]{0:T(1024)S(1)} %copy-done.7, s32[4096]{0:T(1024)S(1)} %get-tuple-element.26, pred[4096]{0:T(1024)(128)(4,1)S(1)} %copy-done.9), kind=kLoop, calls=%fused_computation.22 | loop fusion | flops 2097152 | bytes 562176 | tf_op jit(solution)/shard_map/and | solution.py:55
  55.8 3.0 pad_maximum_fusion
  58.8 9.0 %all-to-all-done.1 = bf16[32,1,64,256]{3,2,1,0:T(8,128)(2,1)} async-done(((bf16[32,1,64,256]{3,2,1,0:T(8,128)(2,1)}), bf16[32,1,64,256]{3,2,1,0:T(8,128)(2,1)}, u32[]{:S(2)}, u32[]{:S(2)}) %all-to-all-start.1) | async-done | bytes 1048608 | tf_op jit(solution)/shard_map/all_to_all | solution.py:101
  67.8 3.1 pad_maximum_fusion.1
  70.9 3.7 %gather_fusion.1 = bf16[64,64,256]{2,1,0:T(8,128)(2,1)} fusion(bf16[64,64,256]{2,1,0:T(8,128)(2,1)} %pad_maximum_fusion, s32[1024]{0:T(1024)} %pad_clamp_fusion), kind=kCustom, calls=%fused_computation.1.clone | custom fusion | bytes 4194560 | tf_op jit(solution)/shard_map/jit(_take)/gather | solution.py:112
  74.6 3.7 %gather_fusion.3 = bf16[64,64,256]{2,1,0:T(8,128)(2,1)} fusion(bf16[64,64,256]{2,1,0:T(8,128)(2,1)} %pad_maximum_fusion.1, s32[1024]{0:T(1024)} %pad_clamp_fusion), kind=kCustom, calls=%fused_computation.3.clone | custom fusion | bytes 4194560 | tf_op jit(solution)/shard_map/jit(_take)/gather | solution.py:111
  78.3 2.7 broadcast_select_fusion
  84.6 1.6 convolution_convert_fusion.1
  86.2 21.4 %reduce-scatter.3.cloned.1.call-done = bf16[32,3584]{1,0:T(8,128)(2,1)} async-done(((bf16[128,3584]{1,0:T(8,128)(2,1)}), bf16[32,3584]{1,0:T(8,128)(2,1)}) %reduce-scatter.3.cloned.1.call-update) | async-done | bytes 229392 | tf_op jit(solution)/shard_map/reduce_scatter | solution.py:162
  112.2 91.5 %all_to_all.15 = bf16[32,32,3584]{2,1,0:T(8,128)(2,1)S(1)} all-to-all(bf16[32,32,3584]{2,1,0:T(8,128)(2,1)S(1)} %stack.2), channel_id=1, replica_groups=mesh['req'=32,'mlp'=4] {'req'}, dimensions={0} | all-to-all | bytes 14680064 | tf_op jit(solution)/shard_map/all_to_all | solution.py:15
  203.7 3.0 copy-done.1
  206.7 4.7 %fusion.62 = f32[1024,448]{0,1:T(8,128)} fusion(bf16[1024,3584]{1,0:T(8,128)(2,1)S(1)} %bitcast.81, bf16[3584,448]{0,1:T(8,128)(2,1)S(1)} %copy-done.17), kind=kOutput, calls=%fused_computation.122 | convolution fusion | flops 3288334336 | bytes 12386304 | tf_op jit(solution)/shard_map/dot_general | solution.py:174
  211.5 13.0 %convolution_convert_fusion = bf16[1024,3584]{1,0:T(8,128)(2,1)} fusion(bf16[448,3584]{1,0:T(8,128)(2,1)S(1)} %copy-done, f32[1024,448]{0,1:T(8,128)} %fusion.62, bf16[1024,3584]{1,0:T(8,128)(2,1)} %bitcast.82, bf16[3584,448]{0,1:T(8,128)(2,1)} %param.37), kind=kOutput, calls=%fused_computation.4 | convolution fusion | flops 6584926208 | bytes 22937600 | tf_op jit(solution)/shard_map/dot_general | solution.py:178
  224.5 85.2 %reduce-scatter.5.cloned.1.call-done = bf16[32,3584]{1,0:T(8,128)(2,1)} async-done(((bf16[1024,3584]{1,0:T(8,128)(2,1)}), bf16[32,3584]{1,0:T(8,128)(2,1)}) %reduce-scatter.5.cloned.1.call-update) | async-done | bytes 229392 | tf_op jit(solution)/shard_map/reduce_scatter | solution.py:177
  310.9 2.0 fusion.31
  (84 shorter events, 20.2 us)
Async XLA Ops:
  7.2 204.3 %copy-start = (bf16[448,3584]{1,0:T(8,128)(2,1)S(1)}, bf16[448,3584]{1,0:T(8,128)(2,1)}, u32[]{:S(2)}) copy-start(bf16[448,3584]{1,0:T(8,128)(2,1)} %param.38) | copy-start | bytes 9633796
  17.6 8.6 %copy-start.19 = (s32[1,64]{1,0:T(1,128)S(1)}, s32[1,64]{1,0:T(1,128)}, u32[]{:S(2)}) copy-start(s32[1,64]{1,0:T(1,128)} %param.25) | copy-start | bytes 772
  17.6 11.5 %copy-start.11 = (s32[1,128]{1,0:T(1,128)S(1)}, s32[1,128]{1,0:T(1,128)}, u32[]{:S(2)}) copy-start(s32[1,128]{1,0:T(1,128)} %param.23) | copy-start | bytes 1540
  17.6 12.2 %copy-start.13 = (s32[1,4]{1,0:T(1,128)S(1)}, s32[1,4]{1,0:T(1,128)}, u32[]{:S(2)}) copy-start(s32[1,4]{1,0:T(1,128)} %param.24) | copy-start | bytes 52
  17.6 14.6 %copy-start.18 = (f32[3584]{0:T(1024)S(1)}, f32[3584]{0:T(1024)}, u32[]{:S(2)}) copy-start(f32[3584]{0:T(1024)} %param.29) | copy-start | bytes 43012
  17.6 26.0 %all-to-all-start = ((bf16[32,1,64,256]{3,2,1,0:T(8,128)(2,1)}), bf16[32,1,64,256]{3,2,1,0:T(8,128)(2,1)}, u32[]{:S(2)}, u32[]{:S(2)}) async-start(bf16[32,1,64,256]{3,2,1,0:T(8,128)(2,1)} %get-tuple-element.20), calls=%async_computation | async-start | bytes 2097152 | tf_op jit(solution)/shard_map/all_to_all | solution.py:102
  26.7 8.1 %copy-start.16 = (bf16[3584,512]{1,0:T(8,128)(2,1)S(1)}, bf16[3584,512]{1,0:T(8,128)(2,1)}, u32[]{:S(2)}) copy-start(bf16[3584,512]{1,0:T(8,128)(2,1)} %param.30) | copy-start | bytes 11010052
  27.3 7.5 %copy-start.4 = (bf16[128,3584]{1,0:T(8,128)(2,1)S(1)}, bf16[128,3584]{1,0:T(8,128)(2,1)}, u32[]{:S(2)}) copy-start(bf16[128,3584]{1,0:T(8,128)(2,1)} %param.22) | copy-start | bytes 2752516
  29.1 7.1 %copy-start.22 = (f32[128]{0:T(128)}, f32[128]{0:T(128)S(1)}, u32[]{:S(2)}) copy-start(f32[128]{0:T(128)S(1)} %add_rsqrt_fusion.3) | copy-start | bytes 1540
  41.3 9.8 %copy-start.7 = (s32[4096]{0:T(1024)S(1)}, s32[4096]{0:T(1024)}, u32[]{:S(2)}) copy-start(s32[4096]{0:T(1024)} %get-tuple-element.25) | copy-start | bytes 49156
  41.3 9.8 %copy-start.9 = (pred[4096]{0:T(1024)(128)(4,1)S(1)}, pred[4096]{0:T(1024)(128)(4,1)}, u32[]{:S(2)}) copy-start(pred[4096]{0:T(1024)(128)(4,1)} %subtract_compare_fusion) | copy-start | bytes 12292
  41.3 9.8 %copy-start.12 = (s32[1,128]{1,0:T(1,128)S(1)}, s32[1,128]{1,0:T(1,128)}, u32[]{:S(2)}) copy-start(s32[1,128]{1,0:T(1,128)} %param.23) | copy-start | bytes 1540
  41.3 9.8 %copy-start.14 = (s32[128]{0:T(128)S(1)}, s32[128]{0:T(128)}, u32[]{:S(2)}) copy-start(s32[128]{0:T(128)} %get-tuple-element.16) | copy-start | bytes 1540
  43.6 39.7 %copy-start.20 = (bf16[128,256]{1,0:T(8,128)(2,1)}, bf16[128,256]{1,0:T(8,128)(2,1)S(1)}, u32[]{:S(2)}) copy-start(bf16[128,256]{1,0:T(8,128)(2,1)S(1)} %convolution_convert_fusion.2) | copy-start | bytes 196612
  43.6 24.2 %all-to-all-start.1 = ((bf16[32,1,64,256]{3,2,1,0:T(8,128)(2,1)}), bf16[32,1,64,256]{3,2,1,0:T(8,128)(2,1)}, u32[]{:S(2)}, u32[]{:S(2)}) async-start(bf16[32,1,64,256]{3,2,1,0:T(8,128)(2,1)} %get-tuple-element.19), calls=%async_computation.1 | async-start | bytes 2097152 | tf_op jit(solution)/shard_map/all_to_all | solution.py:101
  51.1 56.6 %reduce-scatter.3.cloned.1.call-start = ((), (), s32[]{:S(2)}) async-start(), calls=%async_computation.5 | async-start | bytes 1146880 | tf_op jit(solution)/shard_map/reduce_scatter | solution.py:162
  74.6 3.7 %copy-start.15 = (pred[64]{0:T(512)(128)(4,1)S(1)}, pred[64]{0:T(512)(128)(4,1)}, u32[]{:S(2)}) copy-start(pred[64]{0:T(512)(128)(4,1)} %compare_and_fusion) | copy-start | bytes 196
  84.6 24.2 %copy-start.6 = (f32[3584]{0:T(1024)S(1)}, f32[3584]{0:T(1024)}, u32[]{:S(2)}) copy-start(f32[3584]{0:T(1024)} %param.34) | copy-start | bytes 43012
  84.6 25.5 %copy-start.10 = (f32[3584]{0:T(1024)S(1)}, f32[3584]{0:T(1024)}, u32[]{:S(2)}) copy-start(f32[3584]{0:T(1024)} %param.35) | copy-start | bytes 43012
  86.2 223.6 %reduce-scatter.5.cloned.1.call-start = ((), (), s32[]{:S(2)}) async-start(), calls=%async_computation.6 | async-start | bytes 7569408 | tf_op jit(solution)/shard_map/reduce_scatter | solution.py:177
  112.2 94.6 %copy-start.17 = (bf16[3584,448]{0,1:T(8,128)(2,1)S(1)}, bf16[3584,448]{0,1:T(8,128)(2,1)}, u32[]{:S(2)}) copy-start(bf16[3584,448]{0,1:T(8,128)(2,1)} %param.36) | copy-start | bytes 9633796
  203.7 3.0 copy-start.1
  224.5 86.4 %copy-start.3 = (bf16[32,3584]{1,0:T(8,128)(2,1)S(1)}, bf16[32,3584]{1,0:T(8,128)(2,1)}, u32[]{:S(2)}) copy-start(bf16[32,3584]{1,0:T(8,128)(2,1)} %reduce-scatter.3.cloned.1.call-done) | copy-start | bytes 688132
  224.5 86.4 %copy-start.8 = (f32[3584]{0:T(1024)S(1)}, f32[3584]{0:T(1024)}, u32[]{:S(2)}) copy-start(f32[3584]{0:T(1024)} %param.39) | copy-start | bytes 43012
  (3 other events, 5.7 us)
Sparse Core Ops, SparseCore 0:
  86.3 21.2 reduce-scatter.2
  224.6 85.0 reduce-scatter.4
